TPU v7x, 32 devices: a whole 2x2x4 slice. The times are simulated.
32 devices in a mesh: groups: 2 (over y), seq: 4 (over x, core), heads: 4 (over z).
Axes of the slice: x: 2, y: 2, z: 4, core: 2. Of those that a mesh axis runs over, the one named last changes fastest.
Arguments:
- tokens: bfloat16 [4096, 8192], P(('groups', 'seq'), 'heads'), parts along dimension 0, may hold values from -6 to 6
- xz_weight: bfloat16 [8192, 32768], P(None, ('heads', 'seq')), may hold values from -0.0625 to 0.0625
- bc_weight: bfloat16 [8192, 2048], P(None, 'heads'), may hold values from -0.0625 to 0.0625
- step_weight: bfloat16 [8192, 256], P(None, 'heads'), may hold values from -0.0625 to 0.0625
- step_bias: float32 [256], P('heads'), may hold values from -4 to -2
- decay_log: float32 [256], P('heads'), may hold values from -5.3 to -0.7
- skip_gain: float32 [256], P('heads'), may hold values from 0.5 to 2
- conv_weight: float32 [4, 16384], P(None, 'heads'), may hold values from -3 to 3
- conv_bias: float32 [16384], P('heads'), may hold values from -3 to 3
- bc_conv_weight: float32 [4, 2048], replicated, may hold values from -3 to 3
- bc_conv_bias: float32 [2048], replicated, may hold values from -3 to 3
- norm_gain: float32 [16384], P('heads'), may hold values from 0.1 to 1.9
- step_bounds: int32 [32], P('groups'), parts along dimension 0, may hold values from 0 to 2047, as said below
- readers: int32 [32], P('groups'), parts along dimension 0, may hold values from 0 to 3, as said below
Outputs:
- mixed: bfloat16 [4096, 16384], P(('groups', 'seq'), 'heads'), parts along dimension 0
- handoff: bfloat16 [8, 4, 256, 64, 128], P(('groups', 'heads'), None, 'seq'), parts along dimension 0
There are 2 independent parts, one for each index of `groups`. A program takes and returns all parts, laid end to end along the dimension named above; an argument that names none is the same for every part. Nothing has to cross between parts.
Inputs may be any that keep to these rules, and one draw needn't show every extreme that they name: `step_bounds`: boundary j * 4 + i, for i < 4, lies in section j: positions j * 512 to (j + 1) * 512 - 1. The first boundary is at position 0 and the last at 2047. `readers`: among the 4 boundaries of each section every reader appears exactly once.
All inputs are finite; a program needn't handle non-finite values.
Results may differ from a plain program's by a relative error of at most 0.0056.
Values may be sent and summed in bfloat16 or wider, within the bound.
A program may use at most 384 MiB of HBM per device.

v0:
```python
import jax
import jax.numpy as jnp
from jax import lax
from jax.sharding import PartitionSpec as P

H = 256
P_SIZE = 64
N = 128
G = 8
CH = 256
EPSILON = 1e-05
HIGHEST_PRECISION = lax.Precision.HIGHEST


def from_behind(value, axis, steps):
    count = lax.axis_size(axis)
    first, last = (max(0, -steps), min(count, count - steps))
    return lax.ppermute(value, axis, [(source, source + steps) for source in range(first, last)])


def entering(part, axis, combine, identity):
    place = lax.axis_index(axis)
    gathered = jax.tree.map(lambda a: lax.all_gather(a, axis), part)
    state = jax.tree.map(lambda a, e: jnp.zeros_like(a) + jnp.asarray(e, a.dtype), part, identity)

    def one(step, state):
        return combine(
            state, jax.tree.map(lambda a: lax.dynamic_index_in_dim(a, step, 0, False), gathered)
        )

    return lax.fori_loop(0, place, one, state)


def conv_rows(prefix, raw_rows, kernel, shift_bias):
    row_count = raw_rows.shape[0]
    padded = jnp.concatenate([prefix, raw_rows], axis=0).astype(jnp.float32)
    summed = jnp.broadcast_to(shift_bias[None, :], raw_rows.shape)
    for tap_index in range(kernel.shape[0]):
        summed = summed + kernel[tap_index][None, :] * padded[tap_index : tap_index + row_count]
    return jax.nn.silu(summed).astype(jnp.bfloat16)


def shards(
    tokens,
    xz_weight,
    bc_weight,
    step_weight,
    step_bias,
    decay_log,
    skip_gain,
    conv_weight,
    conv_bias,
    bc_conv_weight,
    bc_conv_bias,
    norm_gain,
    step_bounds,
    readers,
):
    head_devices = lax.axis_size("heads")
    section = lax.axis_index("seq")
    head_block = lax.axis_index("heads")
    local_heads = H // head_devices
    per_group = H // G
    local_groups = max(1, local_heads // per_group)
    group_heads = local_heads // local_groups
    first_group = head_block * local_heads // per_group
    gathered = lax.all_gather(tokens, "heads", axis=1, tiled=True)
    row_count = gathered.shape[0]
    xz_rows = jnp.dot(
        gathered,
        lax.all_gather(xz_weight, "seq", axis=1, tiled=True),
        preferred_element_type=jnp.float32,
    ).astype(jnp.bfloat16)
    head_cols = xz_rows.reshape(row_count, local_heads, 2 * P_SIZE)
    inner_raw = head_cols[:, :, :P_SIZE].reshape(row_count, local_heads * P_SIZE)
    gate_raw = head_cols[:, :, P_SIZE:].reshape(row_count, local_groups, group_heads, P_SIZE)
    bc_part = jnp.dot(gathered, bc_weight, preferred_element_type=jnp.float32).astype(jnp.bfloat16)
    step_raw = jnp.dot(gathered, step_weight, preferred_element_type=jnp.float32)
    bc_every = lax.all_gather(bc_part, "heads", axis=1, tiled=True)
    width_bc = local_groups * 2 * N
    bc_mine = lax.dynamic_slice_in_dim(bc_every, first_group * 2 * N, width_bc, 1)
    kernel_bc = lax.dynamic_slice_in_dim(bc_conv_weight, first_group * 2 * N, width_bc, 1)
    shift_bc = lax.dynamic_slice_in_dim(bc_conv_bias, first_group * 2 * N, width_bc, 0)
    taps = conv_weight.shape[0]
    joined = jnp.concatenate([inner_raw, bc_mine], axis=1)
    previous = from_behind(joined[row_count - taps + 1 :], "seq", 1)
    inner_conv = conv_rows(
        previous[:, : local_heads * P_SIZE], inner_raw, conv_weight, conv_bias
    ).reshape(row_count, local_groups, group_heads, P_SIZE)
    bc_conv = conv_rows(previous[:, local_heads * P_SIZE :], bc_mine, kernel_bc, shift_bc).reshape(
        row_count, local_groups, 2 * N
    )
    b_input = bc_conv[:, :, :N]
    c_input = bc_conv[:, :, N:]
    step_size = jax.nn.softplus(step_raw + step_bias[None, :]).reshape(
        row_count, local_groups, group_heads
    )
    decay_rate = -jnp.exp(decay_log).reshape(local_groups, group_heads)[None] * step_size
    blocks = row_count // CH
    causal = lax.broadcasted_iota(jnp.int32, (CH, CH), 0) >= lax.broadcasted_iota(
        jnp.int32, (CH, CH), 1
    )
    running = jnp.zeros((local_groups, group_heads, P_SIZE, N), jnp.float32)
    local_starts = []
    intra_parts = []
    cum_parts = []
    block_totals = []
    for block_index in range(blocks):
        first_row = block_index * CH
        inner_blk = inner_conv[first_row : first_row + CH]
        b_blk = b_input[first_row : first_row + CH]
        c_blk = c_input[first_row : first_row + CH]
        step_blk = step_size[first_row : first_row + CH]
        cum_block = jnp.cumsum(decay_rate[first_row : first_row + CH], axis=0)
        scores = jnp.einsum("tgn,sgn->gts", c_blk, b_blk, preferred_element_type=jnp.float32)
        cum_gap = cum_block[:, None] - cum_block[None, :]
        weight = (
            jnp.where(causal[:, :, None, None], jnp.exp(jnp.minimum(cum_gap, 0.0)), 0.0)
            * step_blk[None]
        )
        mixing = (weight * jnp.transpose(scores, (1, 2, 0))[:, :, :, None]).astype(jnp.bfloat16)
        intra_parts.append(
            jnp.einsum("tsgr,sgrp->tgrp", mixing, inner_blk, preferred_element_type=jnp.float32)
        )
        cum_parts.append(cum_block)
        local_starts.append(running)
        block_total = cum_block[-1]
        block_totals.append(block_total)
        carry_weight = jnp.exp(block_total[None] - cum_block) * step_blk
        weighted = (inner_blk.astype(jnp.float32) * carry_weight[..., None]).astype(jnp.bfloat16)
        running = jnp.exp(block_total)[..., None, None] * running + jnp.einsum(
            "sgrp,sgn->grpn", weighted, b_blk, preferred_element_type=jnp.float32
        )
    section_decay = block_totals[0]
    block_index = 1
    section_decay = section_decay + block_totals[block_index]

    def combine(earlier, later):
        return (earlier[0] + later[0], jnp.exp(later[0])[..., None, None] * earlier[1] + later[1])

    identity = (jnp.zeros_like(section_decay), jnp.zeros_like(running))
    incoming = entering((section_decay, running), "seq", combine, identity)[1]
    global_starts = []
    ssd_parts = []
    prior_decay = jnp.zeros_like(section_decay)
    for block_index in range(blocks):
        start_state = local_starts[block_index] + jnp.exp(prior_decay)[..., None, None] * incoming
        global_starts.append(start_state)
        prior_decay = prior_decay + block_totals[block_index]
        first_row = block_index * CH
        c_blk = c_input[first_row : first_row + CH]
        outer_part = jnp.exp(cum_parts[block_index])[..., None] * jnp.einsum(
            "tgn,grpn->tgrp", c_blk.astype(jnp.float32), start_state, precision=HIGHEST_PRECISION
        )
        ssd_parts.append(intra_parts[block_index] + outer_part)
    ssd = jnp.concatenate(ssd_parts, axis=0) + skip_gain.reshape(local_groups, group_heads)[
        None, :, :, None
    ] * inner_conv.astype(jnp.float32)
    gated = ssd * jax.nn.silu(gate_raw.astype(jnp.float32))
    local_square = jnp.sum(gated * gated, axis=(2, 3))
    placed = lax.dynamic_update_slice_in_dim(
        jnp.zeros((row_count, G), jnp.float32), local_square, first_group, 1
    )
    square_total = lax.psum(placed, "heads")
    square_mean = lax.dynamic_slice_in_dim(square_total, first_group, local_groups, 1) / (
        per_group * P_SIZE
    )
    normed = (
        gated
        * lax.rsqrt(square_mean + EPSILON)[:, :, None, None]
        * norm_gain.reshape(local_groups, group_heads, P_SIZE)[None]
    )
    mixed = normed.astype(jnp.bfloat16).reshape(row_count, local_heads * P_SIZE)
    cum_all = jnp.concatenate(cum_parts, axis=0)
    starts_all = jnp.stack(global_starts, axis=0)
    positions = lax.broadcasted_iota(jnp.int32, (row_count,), 0)
    bound_local = (
        lax.dynamic_slice_in_dim(step_bounds, section * head_devices, head_devices, 0)
        - section * row_count
    )
    reader_local = lax.dynamic_slice_in_dim(readers, section * head_devices, head_devices, 0)
    block_of = bound_local // CH
    cum_at = cum_all[bound_local]
    inside_mask = (positions[None, :] // CH == block_of[:, None]) & (
        positions[None, :] <= bound_local[:, None]
    )
    cum_gap = cum_at[:, None] - cum_all[None]
    bound_weight = (
        jnp.where(inside_mask[:, :, None, None], jnp.exp(jnp.minimum(cum_gap, 0.0)), 0.0)
        * step_size[None]
    )
    bound_weighted = (inner_conv[None].astype(jnp.float32) * bound_weight[..., None]).astype(
        jnp.bfloat16
    )
    inside = jnp.einsum(
        "bsgrp,sgn->bgrpn", bound_weighted, b_input, preferred_element_type=jnp.float32
    )
    states = jnp.exp(cum_at)[..., None, None] * starts_all[block_of] + inside
    inverse = jnp.argsort(reader_local)
    ordered = states[inverse].reshape(head_devices, local_heads, P_SIZE, N).astype(jnp.bfloat16)
    arrived = lax.all_to_all(
        lax.all_to_all(ordered, "heads", split_axis=0, concat_axis=1, tiled=True),
        "seq",
        split_axis=1,
        concat_axis=0,
        tiled=True,
    )
    return (mixed, arrived[None])


def solution(mesh):
    in_specs = (
        P(("groups", "seq"), "heads"),
        P(None, ("heads", "seq")),
        P(None, "heads"),
        P(None, "heads"),
        P("heads"),
        P("heads"),
        P("heads"),
        P(None, "heads"),
        P("heads"),
        P(),
        P(),
        P("heads"),
        P("groups"),
        P("groups"),
    )
    out_specs = (P(("groups", "seq"), "heads"), P(("groups", "heads"), None, "seq", None, None))
    return jax.shard_map(shards, mesh=mesh, in_specs=in_specs, out_specs=out_specs, check_vma=False)
```

profile of v0, /device:TPU:6, one launch (start us, length us, event | category | flops | bytes accessed | tf_op | source)
XLA Modules:
  0.0 1422.9 jit_solution(13541814008040680989)
XLA Ops:
  8.0 152.5 %all-gather.6.cloned.1.call-done = bf16[512,8192]{1,0:T(8,128)(2,1)} async-done(((bf16[512,2048]{1,0:T(8,128)(2,1)}), bf16[512,8192]{1,0:T(8,128)(2,1)}) %all-gather.6.cloned.1.call-update) | async-done | bytes 8388624 | tf_op jit(solution)/shard_map/all_gather | solution.py:67
  160.4 11.0 convolution_convert_fusion.1
  174.6 6.4 compare_select_fusion
  185.7 30.3 %all-gather.10.cloned.1.call-done = bf16[512,2048]{1,0:T(8,128)(2,1)} async-done(((bf16[512,512]{1,0:T(8,128)(2,1)}), bf16[512,2048]{1,0:T(8,128)(2,1)}) %all-gather.10.cloned.1.call-update) | async-done | bytes 2097168 | tf_op jit(solution)/shard_map/all_gather | solution.py:79
  217.0 773.3 %all-gather.8.cloned.1.call-done = bf16[8192,8192]{1,0:T(8,128)(2,1)} async-done(((bf16[8192,2048]{1,0:T(8,128)(2,1)}), bf16[8192,8192]{1,0:T(8,128)(2,1)}) %all-gather.8.cloned.1.call-update) | async-done | bytes 134217744 | tf_op jit(solution)/shard_map/all_gather | solution.py:71
  990.3 79.7 %convolution_convert_fusion = bf16[512,8192]{1,0:T(8,128)(2,1)} fusion(bf16[512,8192]{1,0:T(8,128)(2,1)} %all-gather.6.cloned.1.call-done, bf16[8192,8192]{1,0:T(8,128)(2,1)} %all-gather.8.cloned.1.call-done), kind=kOutput, calls=%fused_computation.11 | convolution fusion | flops 68723671040 | bytes 150994944 | tf_op jit(solution)/shard_map/dot_general | solution.py:69
  1070.1 12.0 copy.125
  1082.1 7.6 slice_convert_fusion
  1089.6 6.3 copy.101
  1108.6 10.7 multiply_convert_fusion.6
  1127.3 5.1 all_gather.22
  1134.6 48.9 %all-gather.12.cloned.1.call-done = f32[8,32,64,128]{3,2,1,0:T(8,128)} async-done(((f32[2,32,64,128]{3,2,1,0:T(8,128)}), f32[8,32,64,128]{3,2,1,0:T(8,128)}) %all-gather.12.cloned.1.call-update) | async-done | bytes 8388624 | tf_op jit(solution)/shard_map/all_gather | solution.py:23
  1190.0 5.5 fusion.42
  1201.6 6.8 gather_fusion.1
  1208.5 7.2 fusion.31
  1215.8 6.8 fusion.32
  1222.7 14.6 %fusion.15 = (f32[512,2]{0,1:T(2,128)S(1)}, f32[512,4096]{0,1:T(8,128)}) fusion(f32[256,2,32,64]{0,3,2,1:T(8,128)S(1)} %fusion.31, f32[256,2,32,64]{0,3,2,1:T(8,128)} %fusion.32, f32[512,2,32,64]{0,3,2,1:T(8,128)} %bitcast.150, f32[2,32]{1,0:T(2,128)S(1)} %mul.366, f32[515,4096]{0,1:T(8,128)S(1)} %bitcast.147, f32[4096]{0:T(1024)S(1)} %bitcast.176, ...), kind=kLoop, calls=%fused_computation.30 | loop fusion | flops 50330624 | bytes 58806528 | tf_op jit(solution)/shard_map/reduce_sum | solution.py:160
  1237.3 9.6 bitcast_add_fusion.1
  1247.0 5.3 gather_fusion.2
  1252.3 99.6 %all_to_all.24 = bf16[4,64,64,128]{3,2,1,0:T(8,128)(2,1)} all-to-all(bf16[4,64,64,128]{3,2,1,0:T(8,128)(2,1)} %bitcast.155), channel_id=1, replica_groups=mesh['groups'=2,'seq'=4,'heads'=4] {'heads'}, dimensions={0} | all-to-all | bytes 8388608 | tf_op jit(solution)/shard_map/all_to_all | solution.py:202
  1357.0 17.2 %psum.7 = f32[512,8]{0,1:T(8,128)S(1)} all-reduce(f32[512,8]{0,1:T(8,128)S(1)} %dynamic_update_slice.3), channel_id=1, replica_groups=mesh['groups'=2,'seq'=4,'heads'=4] {'heads'}, use_global_device_ids=true, to_apply=%region_7.8 | all-reduce | flops 4096 | bytes 32768 | tf_op jit(solution)/shard_map/psum | solution.py:164
  1374.3 30.4 %fusion.12 = bf16[512,4096]{0,1:T(8,128)(2,1)} fusion(f32[256,4096]{0,1:T(8,128)} %bitcast.156, f32[256,4096]{0,1:T(8,128)} %bitcast.157, f32[512,64,64]{0,2,1:T(8,128)} %get-tuple-element.76, f32[4096]{0:T(1024)S(1)} %copy-done.29, f32[512,2]{0,1:T(2,128)S(1)} %add_rsqrt_fusion, f32[4096]{0:T(1024)S(1)} %mul.368, f32[515,4096]{0,1:T(8,128)} %copy-done.2, ...), kind=kLoop, calls=%fused_computation.26 | loop fusion | flops 52428800 | bytes 54644736 | tf_op jit(solution)/shard_map/convert_element_type | solution.py:173
  1404.6 6.3 copy.119
  1411.0 5.2 copy.181
  (168 shorter events, 53.7 us)
Async XLA Ops:
  7.2 167.3 %copy-start = (bf16[8192,64]{0,1:T(8,128)(2,1)S(1)}, bf16[8192,64]{0,1:T(8,128)(2,1)}, u32[]{:S(2)}) copy-start(bf16[8192,64]{0,1:T(8,128)(2,1)} %param.19) | copy-start | bytes 3145732
  7.2 153.3 %all-gather.6.cloned.1.call-start = ((), (), s32[]{:S(2)}) async-start(), calls=%async_computation.2 | async-start | bytes 10485760 | tf_op jit(solution)/shard_map/all_gather | solution.py:67
  7.9 208.0 %all-gather.10.cloned.1.call-start = ((), (), s32[]{:S(2)}) async-start(), calls=%async_computation.4 | async-start | bytes 2621440 | tf_op jit(solution)/shard_map/all_gather | solution.py:79
  171.5 818.8 %all-gather.8.cloned.1.call-start = ((), (), s32[]{:S(2)}) async-start(), calls=%async_computation.3 | async-start | bytes 167772160 | tf_op jit(solution)/shard_map/all_gather | solution.py:71
  172.3 1011.3 %all-gather.12.cloned.1.call-start = ((), (), s32[]{:S(2)}) async-start(), calls=%async_computation.5 | async-start | bytes 10485760 | tf_op jit(solution)/shard_map/all_gather | solution.py:23
  174.5 934.0 %copy-start.16 = (f32[1,4096]{1,0:T(1,128)}, f32[1,4096]{1,0:T(1,128)S(1)}, u32[]{:S(2)}) copy-start(f32[1,4096]{1,0:T(1,128)S(1)} %get-tuple-element.96) | copy-start | bytes 49156
  174.5 934.0 %copy-start.18 = (f32[1,4096]{1,0:T(1,128)}, f32[1,4096]{1,0:T(1,128)S(1)}, u32[]{:S(2)}) copy-start(f32[1,4096]{1,0:T(1,128)S(1)} %get-tuple-element.97) | copy-start | bytes 49156
  174.5 934.0 %copy-start.20 = (f32[1,4096]{1,0:T(1,128)}, f32[1,4096]{1,0:T(1,128)S(1)}, u32[]{:S(2)}) copy-start(f32[1,4096]{1,0:T(1,128)S(1)} %get-tuple-element.98) | copy-start | bytes 49156
  184.2 885.8 %copy-start.12 = (f32[256,64]{0,1:T(8,128)}, f32[256,64]{0,1:T(8,128)S(1)}, u32[]{:S(2)}) copy-start(f32[256,64]{0,1:T(8,128)S(1)} %get-tuple-element.85) | copy-start | bytes 196612
  184.3 885.8 %copy-start.14 = (f32[256,64]{0,1:T(8,128)}, f32[256,64]{0,1:T(8,128)S(1)}, u32[]{:S(2)}) copy-start(f32[256,64]{0,1:T(8,128)S(1)} %get-tuple-element.84) | copy-start | bytes 196612
  1096.8 5.3 collective-permute-start
  1100.1 21.6 %copy-start.27 = (f32[2,32]{1,0:T(2,128)}, f32[2,32]{1,0:T(2,128)S(1)}, u32[]{:S(2)}) copy-start(f32[2,32]{1,0:T(2,128)S(1)} %get-tuple-element.104) | copy-start | bytes 772
  1103.1 29.5 %copy-start.10 = (bf16[512,2,256]{2,1,0:T(2,128)(2,1)}, bf16[512,2,256]{2,1,0:T(2,128)(2,1)S(1)}, u32[]{:S(2)}) copy-start(bf16[512,2,256]{2,1,0:T(2,128)(2,1)S(1)} %reshape.225) | copy-start | bytes 1572868
  1108.5 10.8 copy-start.2
  1208.5 7.2 copy-start.6
  1208.5 7.2 copy-start.9
  1208.5 7.2 copy-start.11
  1208.5 7.2 copy-start.13
  1208.5 7.2 copy-start.25
  1215.7 7.0 copy-start.4
  1222.7 14.6 %slice-start.3 = ((bf16[512,2,256]{2,1,0:T(2,128)(2,1)}), bf16[512,2,128]{2,1,0:T(2,128)(2,1)S(1)}, s32[]{:S(2)}) async-start(bf16[512,2,256]{2,1,0:T(2,128)(2,1)} %copy-done.10), calls=%async_computation.9 | async-start | bytes 524288 | tf_op jit(solution)/shard_map/slice | solution.py:93
  1252.3 121.9 %copy-start.29 = (f32[4096]{0:T(1024)S(1)}, f32[4096]{0:T(1024)}, u32[]{:S(2)}) copy-start(f32[4096]{0:T(1024)} %param.27) | copy-start | bytes 49156
  1351.9 59.1 %all-to-all-start.1 = ((bf16[1,256,64,128]{3,2,0,1:T(8,128)(2,1)}), bf16[1,256,64,128]{3,2,0,1:T(8,128)(2,1)}, u32[]{:S(2)}, u32[]{:S(2)}) async-start(bf16[1,256,64,128]{3,2,0,1:T(8,128)(2,1)} %bitcast.154), calls=%async_computation.1 | async-start | bytes 8388608 | tf_op jit(solution)/shard_map/all_to_all | solution.py:201
  1374.2 41.9 %copy-start.1 = (bf16[8192,64]{0,1:T(8,128)(2,1)S(1)}, bf16[8192,64]{0,1:T(8,128)(2,1)}, u32[]{:S(2)}) copy-start(bf16[8192,64]{0,1:T(8,128)(2,1)} %param.19) | copy-start | bytes 3145732
  (22 other events, 111.7 us)
Sparse Core Ops, SparseCore 0:
  9.6 150.8 all-gather.5
  171.6 44.2 all-gather.9
  217.5 772.7 all-gather.7
  1125.2 58.2 all-gather.11
where the time goes:
time: 1430 us; the launch traced here: 1420 us
  waiting for transfers between devices  1010 us (71%)
  matrix products  135 us (9%)
  blocking collectives  122 us (9%)
  other arithmetic  83.8 us (6%)
  local copies, waits for them, and re-layouts  50.9 us (4%)
  between operations  14.8 us (1%)
    all_gather x1, waiting for transfers between devices, shards(): lax.all_gather(xz_weight, 'seq', axis=1, tiled=True)  773 us
    all_gather x1, waiting for transfers between devices, shards(): gathered = lax.all_gather(tokens, 'heads', axis=1, tiled=True)  152 us
    all_to_all x1, blocking collectives, shards(): lax.all_to_all(ordered, 'heads', split_axis=0, concat_axis=1, tiled=True)  99.6 us
    dot_general x1, matrix products, shards(): jnp.dot(gathered, lax.all_gather(xz_weight, 'seq', axis=1, tiled=True), p...  79.7 us
    all_gather x1, waiting for transfers between devices, entering(): gathered = jax.tree.map(lambda a: lax.all_gather(a, axis), part)  48.9 us
    convert_element_type x1, other arithmetic, shards(): mixed = normed.astype(jnp.bfloat16).reshape(row_count, local_heads * P_SIZE)  30.4 us
    all_gather x1, waiting for transfers between devices, shards(): bc_every = lax.all_gather(bc_part, 'heads', axis=1, tiled=True)  30.3 us
  transfers between devices with their start and end apart: 6, of which 5 were waited for; matrix products, arithmetic and copies ran while one was open for 4% of the time, Pallas kernels for 0%

commit v1 on v0

--- a/solution.py
+++ b/solution.py
@@ -198,12 +198,20 @@
     states = jnp.exp(cum_at)[..., None, None] * starts_all[block_of] + inside
     inverse = jnp.argsort(reader_local)
     ordered = states[inverse].reshape(head_devices, local_heads, P_SIZE, N).astype(jnp.bfloat16)
-    arrived = lax.all_to_all(
-        lax.all_to_all(ordered, "heads", split_axis=0, concat_axis=1, tiled=True),
-        "seq",
-        split_axis=1,
-        concat_axis=0,
-        tiled=True,
+    arrived = jnp.concatenate(
+        lax.all_to_all(
+            jnp.stack(
+                jnp.split(
+                    lax.all_to_all(ordered, "heads", split_axis=0, concat_axis=1, tiled=True),
+                    lax.axis_size("seq"),
+                    axis=1,
+                )
+            ),
+            "seq",
+            0,
+            0,
+        ),
+        axis=0,
     )
     return (mixed, arrived[None])
 

time: 1430 us -> 1430 us (level)
  no operation moved by 1% of the time
where the time goes in v1:
time: 1430 us
  waiting for transfers between devices  1010 us (71%)
  matrix products  135 us (9%)
  blocking collectives  121 us (8%)
  other arithmetic  86 us (6%)
  local copies, waits for them, and re-layouts  51.9 us (4%)
  between operations  14.8 us (1%)
    all_gather x1, waiting for transfers between devices, shards(): lax.all_gather(xz_weight, 'seq', axis=1, tiled=True)  773 us
    all_gather x1, waiting for transfers between devices, shards(): gathered = lax.all_gather(tokens, 'heads', axis=1, tiled=True)  152 us
    all_to_all x1, blocking collectives, shards(): lax.all_to_all(ordered, 'heads', split_axis=0, concat_axis=1, tiled=True)  98.4 us
    dot_general x1, matrix products, shards(): jnp.dot(gathered, lax.all_gather(xz_weight, 'seq', axis=1, tiled=True), p...  79.7 us
    all_gather x1, waiting for transfers between devices, entering(): gathered = jax.tree.map(lambda a: lax.all_gather(a, axis), part)  49 us
    convert_element_type x1, other arithmetic, shards(): mixed = normed.astype(jnp.bfloat16).reshape(row_count, local_heads * P_SIZE)  30.4 us
    all_gather x1, waiting for transfers between devices, shards(): bc_every = lax.all_gather(bc_part, 'heads', axis=1, tiled=True)  30.2 us
  transfers between devices with their start and end apart: 6, of which 5 were waited for; matrix products, arithmetic and copies ran while one was open for 4% of the time, Pallas kernels for 0%

profile of v1, /device:TPU:6, one launch (start us, length us, event | category | flops | bytes accessed | tf_op | source)
XLA Modules:
  0.0 1425.0 jit_solution(5924007737416059437)
XLA Ops:
  8.0 152.5 %all-gather.6.cloned.1.call-done = bf16[512,8192]{1,0:T(8,128)(2,1)} async-done(((bf16[512,2048]{1,0:T(8,128)(2,1)}), bf16[512,8192]{1,0:T(8,128)(2,1)}) %all-gather.6.cloned.1.call-update) | async-done | bytes 8388624 | tf_op jit(solution)/shard_map/all_gather | solution.py:67
  160.4 11.0 convolution_convert_fusion.1
  174.6 6.4 compare_select_fusion
  185.7 30.2 %all-gather.10.cloned.1.call-done = bf16[512,2048]{1,0:T(8,128)(2,1)} async-done(((bf16[512,512]{1,0:T(8,128)(2,1)}), bf16[512,2048]{1,0:T(8,128)(2,1)}) %all-gather.10.cloned.1.call-update) | async-done | bytes 2097168 | tf_op jit(solution)/shard_map/all_gather | solution.py:79
  217.0 773.3 %all-gather.8.cloned.1.call-done = bf16[8192,8192]{1,0:T(8,128)(2,1)} async-done(((bf16[8192,2048]{1,0:T(8,128)(2,1)}), bf16[8192,8192]{1,0:T(8,128)(2,1)}) %all-gather.8.cloned.1.call-update) | async-done | bytes 134217744 | tf_op jit(solution)/shard_map/all_gather | solution.py:71
  990.3 79.7 %convolution_convert_fusion = bf16[512,8192]{1,0:T(8,128)(2,1)} fusion(bf16[512,8192]{1,0:T(8,128)(2,1)} %all-gather.6.cloned.1.call-done, bf16[8192,8192]{1,0:T(8,128)(2,1)} %all-gather.8.cloned.1.call-done), kind=kOutput, calls=%fused_computation.11 | convolution fusion | flops 68723671040 | bytes 150994944 | tf_op jit(solution)/shard_map/dot_general | solution.py:69
  1070.1 12.0 copy.134
  1082.1 7.6 slice_convert_fusion
  1089.6 6.3 copy.110
  1108.6 10.7 multiply_convert_fusion.6
  1127.2 5.1 all_gather.22
  1134.5 49.0 %all-gather.12.cloned.1.call-done = f32[8,32,64,128]{3,2,1,0:T(8,128)} async-done(((f32[2,32,64,128]{3,2,1,0:T(8,128)}), f32[8,32,64,128]{3,2,1,0:T(8,128)}) %all-gather.12.cloned.1.call-update) | async-done | bytes 8388624 | tf_op jit(solution)/shard_map/all_gather | solution.py:23
  1190.0 5.5 fusion.42
  1201.7 6.8 gather_fusion.1
  1208.5 7.2 fusion.31
  1215.8 6.8 fusion.32
  1222.8 14.6 %fusion.15 = (f32[512,2]{0,1:T(2,128)S(1)}, f32[512,4096]{0,1:T(8,128)}) fusion(f32[256,2,32,64]{0,3,2,1:T(8,128)S(1)} %fusion.31, f32[256,2,32,64]{0,3,2,1:T(8,128)} %fusion.32, f32[512,2,32,64]{0,3,2,1:T(8,128)} %bitcast.158, f32[2,32]{1,0:T(2,128)S(1)} %mul.366, f32[515,4096]{0,1:T(8,128)S(1)} %bitcast.155, f32[4096]{0:T(1024)S(1)} %bitcast.184, ...), kind=kLoop, calls=%fused_computation.30 | loop fusion | flops 50330624 | bytes 58806528 | tf_op jit(solution)/shard_map/reduce_sum | solution.py:160
  1237.4 9.6 bitcast_add_fusion.1
  1247.0 5.3 gather_fusion.2
  1252.3 98.4 %all_to_all.17 = bf16[4,64,64,128]{3,2,1,0:T(8,128)(2,1)S(1)} all-to-all(bf16[4,64,64,128]{3,2,1,0:T(8,128)(2,1)} %bitcast.163), channel_id=1, replica_groups=mesh['groups'=2,'seq'=4,'heads'=4] {'heads'}, dimensions={0} | all-to-all | bytes 8388608 | tf_op jit(solution)/shard_map/all_to_all | solution.py:205
  1359.2 17.2 %psum.7 = f32[512,8]{0,1:T(8,128)S(1)} all-reduce(f32[512,8]{0,1:T(8,128)S(1)} %dynamic_update_slice.3), channel_id=1, replica_groups=mesh['groups'=2,'seq'=4,'heads'=4] {'heads'}, use_global_device_ids=true, to_apply=%region_7.8 | all-reduce | flops 4096 | bytes 32768 | tf_op jit(solution)/shard_map/psum | solution.py:164
  1376.4 30.4 %fusion.12 = bf16[512,4096]{0,1:T(8,128)(2,1)} fusion(f32[256,4096]{0,1:T(8,128)} %bitcast.164, f32[256,4096]{0,1:T(8,128)} %bitcast.165, f32[512,64,64]{0,2,1:T(8,128)} %get-tuple-element.76, f32[4096]{0:T(1024)S(1)} %copy-done.29, f32[512,2]{0,1:T(2,128)S(1)} %add_rsqrt_fusion, f32[4096]{0:T(1024)S(1)} %mul.368, f32[515,4096]{0,1:T(8,128)} %copy-done.2, ...), kind=kLoop, calls=%fused_computation.26 | loop fusion | flops 52428800 | bytes 54644736 | tf_op jit(solution)/shard_map/convert_element_type | solution.py:173
  1406.8 6.3 copy.128
  1413.1 5.2 copy.190
  (174 shorter events, 57.0 us)
Async XLA Ops:
  7.2 167.3 %copy-start = (bf16[8192,64]{0,1:T(8,128)(2,1)S(1)}, bf16[8192,64]{0,1:T(8,128)(2,1)}, u32[]{:S(2)}) copy-start(bf16[8192,64]{0,1:T(8,128)(2,1)} %param.19) | copy-start | bytes 3145732
  7.2 153.3 %all-gather.6.cloned.1.call-start = ((), (), s32[]{:S(2)}) async-start(), calls=%async_computation.2 | async-start | bytes 10485760 | tf_op jit(solution)/shard_map/all_gather | solution.py:67
  7.9 208.0 %all-gather.10.cloned.1.call-start = ((), (), s32[]{:S(2)}) async-start(), calls=%async_computation.4 | async-start | bytes 2621440 | tf_op jit(solution)/shard_map/all_gather | solution.py:79
  171.5 818.8 %all-gather.8.cloned.1.call-start = ((), (), s32[]{:S(2)}) async-start(), calls=%async_computation.3 | async-start | bytes 167772160 | tf_op jit(solution)/shard_map/all_gather | solution.py:71
  172.3 1011.3 %all-gather.12.cloned.1.call-start = ((), (), s32[]{:S(2)}) async-start(), calls=%async_computation.5 | async-start | bytes 10485760 | tf_op jit(solution)/shard_map/all_gather | solution.py:23
  174.5 934.0 %copy-start.16 = (f32[1,4096]{1,0:T(1,128)}, f32[1,4096]{1,0:T(1,128)S(1)}, u32[]{:S(2)}) copy-start(f32[1,4096]{1,0:T(1,128)S(1)} %get-tuple-element.100) | copy-start | bytes 49156
  174.5 934.0 %copy-start.18 = (f32[1,4096]{1,0:T(1,128)}, f32[1,4096]{1,0:T(1,128)S(1)}, u32[]{:S(2)}) copy-start(f32[1,4096]{1,0:T(1,128)S(1)} %get-tuple-element.101) | copy-start | bytes 49156
  174.5 934.0 %copy-start.20 = (f32[1,4096]{1,0:T(1,128)}, f32[1,4096]{1,0:T(1,128)S(1)}, u32[]{:S(2)}) copy-start(f32[1,4096]{1,0:T(1,128)S(1)} %get-tuple-element.102) | copy-start | bytes 49156
  184.2 885.8 %copy-start.12 = (f32[256,64]{0,1:T(8,128)}, f32[256,64]{0,1:T(8,128)S(1)}, u32[]{:S(2)}) copy-start(f32[256,64]{0,1:T(8,128)S(1)} %get-tuple-element.89) | copy-start | bytes 196612
  184.3 885.8 %copy-start.14 = (f32[256,64]{0,1:T(8,128)}, f32[256,64]{0,1:T(8,128)S(1)}, u32[]{:S(2)}) copy-start(f32[256,64]{0,1:T(8,128)S(1)} %get-tuple-element.88) | copy-start | bytes 196612
  1096.8 5.3 collective-permute-start
  1100.1 21.6 %copy-start.27 = (f32[2,32]{1,0:T(2,128)}, f32[2,32]{1,0:T(2,128)S(1)}, u32[]{:S(2)}) copy-start(f32[2,32]{1,0:T(2,128)S(1)} %get-tuple-element.108) | copy-start | bytes 772
  1103.1 29.4 %copy-start.10 = (bf16[512,2,256]{2,1,0:T(2,128)(2,1)}, bf16[512,2,256]{2,1,0:T(2,128)(2,1)S(1)}, u32[]{:S(2)}) copy-start(bf16[512,2,256]{2,1,0:T(2,128)(2,1)S(1)} %reshape.222) | copy-start | bytes 1572868
  1108.6 10.8 copy-start.2
  1125.2 97.4 %copy-start.32 = (f32[2,32]{1,0:T(2,128)}, f32[2,32]{1,0:T(2,128)S(1)}, u32[]{:S(2)}) copy-start(f32[2,32]{1,0:T(2,128)S(1)} %mul.366) | copy-start | bytes 772
  1208.5 7.2 copy-start.6
  1208.5 7.2 copy-start.9
  1208.5 7.2 copy-start.11
  1208.5 7.2 copy-start.13
  1208.5 7.2 copy-start.25
  1222.7 14.6 %slice-start.3 = ((bf16[512,2,256]{2,1,0:T(2,128)(2,1)}), bf16[512,2,128]{2,1,0:T(2,128)(2,1)S(1)}, s32[]{:S(2)}) async-start(bf16[512,2,256]{2,1,0:T(2,128)(2,1)} %copy-done.10), calls=%async_computation.9 | async-start | bytes 524288 | tf_op jit(solution)/shard_map/slice | solution.py:93
  1351.7 24.7 %copy-start.29 = (f32[4096]{0:T(1024)S(1)}, f32[4096]{0:T(1024)}, u32[]{:S(2)}) copy-start(f32[4096]{0:T(1024)} %param.27) | copy-start | bytes 49156
  1354.0 59.1 %all-to-all-start.1 = ((bf16[4,1,64,64,128]{4,3,2,1,0:T(8,128)(2,1)}), bf16[4,1,64,64,128]{4,3,2,1,0:T(8,128)(2,1)}, u32[]{:S(2)}, u32[]{:S(2)}) async-start(bf16[4,1,64,64,128]{4,3,2,1,0:T(8,128)(2,1)} %pad_maximum_fusion.1), calls=%async_computation.1 | async-start | bytes 8388608 | tf_op jit(solution)/shard_map/all_to_all | solution.py:202
  1376.4 41.9 %copy-start.1 = (bf16[8192,64]{0,1:T(8,128)(2,1)S(1)}, bf16[8192,64]{0,1:T(8,128)(2,1)}, u32[]{:S(2)}) copy-start(bf16[8192,64]{0,1:T(8,128)(2,1)} %param.19) | copy-start | bytes 3145732
  (24 other events, 125.9 us)
Sparse Core Ops, SparseCore 0:
  9.6 150.8 all-gather.5
  171.6 44.2 all-gather.9
  217.5 772.7 all-gather.7
  1125.3 58.2 all-gather.11
